TPU v7x, 32 devices: a whole 2x2x4 slice. The times are simulated.
32 devices in a mesh: row: 4 (over x, core), col: 2 (over y), layer: 4 (over z).
Axes of the slice: x: 2, y: 2, z: 4, core: 2. Of those that a mesh axis runs over, the one named last changes fastest.
Arguments:
- density_matrix: bfloat16 [2048, 2048], P('row', 'col'), may hold values from -3 to 3
- block_mask: int32 [32, 32], P('row', 'col'), may hold values 0 or 1
- intersection_weights: float32 [2048], P(('col', 'layer')), may hold values from -0.125 to 0.125
- exponents: float32 [2048], P('row'), may hold values from 0.5 to 8
- anchor_x: int32 [32], P('row'), may hold values from 0 to 31
- anchor_y: int32 [32], P('row'), may hold values from 0 to 127, as said below
- anchor_z: int32 [32], P('row'), may hold values from 0 to 127
Outputs:
- squared: bfloat16 [2048, 2048], P('row', ('col', 'layer'))
- density: float32 [128, 128, 128], P('row', ('col', 'layer'))
Inputs may be any that keep to these rules, and one draw needn't show every extreme that they name: `anchor_y`: block row a starts in the second dimension between (a mod (8)) * 16 and that plus 16 - 1.
All inputs are finite; a program needn't handle non-finite values. No bound on the sum of `block_mask` on one device may be relied on, other than what follows from the above.
Results may differ from a plain program's by a relative error of at most 0.0055.
Values may be sent and summed in bfloat16 or wider, within the bound.
A program may use at most 64 MiB of HBM per device.

v0:
```python
import jax
import jax.numpy as jnp
from jax import lax
from jax.sharding import PartitionSpec as P

BLOCK = 64
TILE = 16
SX = 32
SY = 16
GZ = 128
grid_step_sq = 0.0625


def broadcast(block, axis, source):
    block = jnp.where(lax.axis_index(axis) == source, block, jnp.zeros_like(block))
    return lax.psum(block, axis)


def shifted(block, axis, distance):
    devices = range(lax.axis_size(axis))
    route = [((i - distance) % len(devices), i) for i in devices]
    return lax.ppermute(block, axis, route)


def local(
    density_matrix, block_mask, intersection_weights, exponents, anchor_x, anchor_y, anchor_z
):
    row_count = lax.axis_size("row")
    col_count = lax.axis_size("col")
    layer_count = lax.axis_size("layer")
    rows_here = density_matrix.shape[0]
    cols_here = density_matrix.shape[1]
    col_ratio = row_count // col_count
    layer_at = lax.axis_index("layer")
    wide_mask = jnp.repeat(jnp.repeat(block_mask, BLOCK, 0), BLOCK, 1)
    masked = jnp.where(wide_mask > 0, density_matrix, jnp.zeros_like(density_matrix))
    width = cols_here // layer_count
    own_cols = lax.dynamic_slice_in_dim(masked, layer_at * width, width, 1)
    running = jnp.zeros((rows_here, width), jnp.float32)
    for inner_at in range(row_count):
        left_part = lax.dynamic_slice_in_dim(masked, inner_at % col_ratio * rows_here, rows_here, 1)
        left_part = broadcast(left_part, "col", inner_at // col_ratio)
        right_part = broadcast(own_cols, "row", inner_at)
        running = running + jnp.dot(left_part, right_part, preferred_element_type=jnp.float32)
    squared = running.astype(jnp.bfloat16)
    partial_charges = jnp.dot(running, intersection_weights, precision=lax.Precision.HIGHEST)
    charges = lax.psum(partial_charges, ("col", "layer"))
    atom_count = anchor_x.shape[0]
    y_index = lax.axis_index("col") * layer_count + layer_at
    offsets = jnp.arange(TILE, dtype=jnp.int32)
    centre = offsets.astype(jnp.float32) - 7.5
    atom_charges = charges.reshape(atom_count, BLOCK)
    decay_rates = exponents.reshape(atom_count, BLOCK)
    profiles = jnp.exp(-decay_rates[:, :, None] * grid_step_sq * centre[None, None, :] ** 2)
    all_tiles = jnp.einsum(
        "ak,akx,aky,akz->axyz",
        atom_charges,
        profiles,
        profiles,
        profiles,
        precision=lax.Precision.HIGHEST,
    )

    def deposit(atom_at, buffer):
        start_y = anchor_y[atom_at] - y_index * SY
        is_owned = (start_y >= 0) & (start_y < SY)
        start_y = jnp.where(is_owned, start_y, 0)
        weight = jnp.where(is_owned, 1.0, 0.0).astype(jnp.float32)
        tile_values = lax.dynamic_index_in_dim(all_tiles, atom_at, 0, keepdims=False)
        start_x = anchor_x[atom_at]
        start_z = anchor_z[atom_at]
        current = lax.dynamic_slice(buffer, (start_x, start_y, start_z), (TILE, TILE, TILE))
        return lax.dynamic_update_slice(
            buffer, current + weight * tile_values, (start_x, start_y, start_z)
        )

    buffer = lax.fori_loop(
        0, atom_count, deposit, jnp.zeros((SX + TILE, SY + TILE, GZ + TILE), jnp.float32)
    )
    buffer = buffer[:, :, :GZ].at[:, :, :TILE].add(buffer[:, :, GZ:])
    rim_x = buffer[SX:]
    came_x = shifted(rim_x.astype(jnp.bfloat16), "row", 1).astype(rim_x.dtype)
    base = buffer[:SX].at[:TILE].add(came_x)
    rim_y = base[:, SY:]
    came_y = shifted(rim_y.astype(jnp.bfloat16), ("col", "layer"), 1).astype(rim_y.dtype)
    density = base[:, :SY].at[:, :TILE].add(came_y)
    return (squared, density)


def solution(mesh):
    return jax.shard_map(
        local,
        mesh=mesh,
        in_specs=(
            P("row", "col"),
            P("row", "col"),
            P(("col", "layer")),
            P("row"),
            P("row"),
            P("row"),
            P("row"),
        ),
        out_specs=(P("row", ("col", "layer")), P("row", ("col", "layer"), None)),
        check_vma=False,
    )
```

profile of v0, /device:TPU:0, one launch (start us, length us, event | category | flops | bytes accessed | tf_op | source)
XLA Modules:
  0.0 261.5 jit_solution(14411166556518656421)
XLA Ops:
  7.2 1.5 copy.11
  9.2 1.1 broadcast_select_fusion.4
  10.3 1.4 broadcast_select_fusion
  11.7 0.6 copy-done.7
  12.5 37.8 %all-reduce.5.cloned.1.call-done = (bf16[512,256]{0,1:T(8,128)(2,1)}, bf16[512,256]{0,1:T(8,128)(2,1)}, bf16[512,256]{0,1:T(8,128)(2,1)}, bf16[512,256]{0,1:T(8,128)(2,1)}) async-done(((bf16[512,256]{0,1:T(8,128)(2,1)}, bf16[512,256]{0,1:T(8,128)(2,1)}, bf16[512,256]{0,1:T(8,128)(2,1)}, bf16[512,256]{0,1:T(8,128)(2,1)}), (bf16[512,256]{0,1:T(8,128)(2,1)}, bf16[512,256]{0,1:T(8,128)(2,1)}, ...) | async-done | bytes 1048592 | tf_op jit(solution)/shard_map/psum | solution.py:16
  50.3 66.0 %all-reduce.7.cloned.1.call-done = (bf16[512,512]{0,1:T(8,128)(2,1)}, bf16[512,512]{0,1:T(8,128)(2,1)}, bf16[512,512]{0,1:T(8,128)(2,1)}, bf16[512,512]{0,1:T(8,128)(2,1)}) async-done(((bf16[512,512]{0,1:T(8,128)(2,1)}, bf16[512,512]{0,1:T(8,128)(2,1)}, bf16[512,512]{0,1:T(8,128)(2,1)}, bf16[512,512]{0,1:T(8,128)(2,1)}), (bf16[512,512]{0,1:T(8,128)(2,1)}, bf16[512,512]{0,1:T(8,128)(2,1)}, ...) | async-done | bytes 2097168 | tf_op jit(solution)/shard_map/psum | solution.py:16
  116.3 1.6 fusion.8
  117.9 1.4 convolution_add_fusion.2
  119.7 1.0 fusion.7
  121.4 20.6 %psum.71 = f32[8,64]{1,0:T(8,128)S(1)} all-reduce(f32[8,64]{1,0:T(8,128)S(1)} %reshape.127), channel_id=1, replica_groups=mesh['row'=4,'col'=2,'layer'=4] {'col','layer'}, use_global_device_ids=true, to_apply=%region_8.9 | all-reduce | flops 512 | bytes 4096 | tf_op jit(solution)/shard_map/psum | solution.py:47
  141.9 1.1 convolution_bitcast_fusion
  143.2 96.2 %while.19 = (s32[]{:T(128)}, f32[48,32,144]{2,1,0:T(8,128)S(1)}, s32[8]{0:T(128)S(1)}, s32[8]{0:T(128)S(1)}, s32[]{:T(128)}, /*index=5*/s32[8]{0:T(128)S(1)}, f3...) while((s32[]{:T(128)}, f32[48,32,144]{2,1,0:T(8,128)S(1)}, ...), condition=%wide.region_10.11_spmd, body=%wide.region_9.10_spmd.sunk | while | flops 8209 | bytes 147826 | solution.py:77
  143.4 0.6 dynamic_slice.79
  145.9 0.6 dynamic_slice.80
  147.2 0.6 dynamic_slice.81
  149.8 5.4 %dynamic_update_slice.10 = f32[48,32,144]{2,1,0:T(8,128)S(1)} dynamic-update-slice(f32[48,32,144]{2,1,0:T(8,128)S(1)} %get-tuple-element.322, f32[16,16,16]{2,1,0:T(8,128)S(1)} %bitcast_add_fusion.2, s32[]{:T(128)S(6)} %select_n.154, s32[]{:T(128)S(6)} %select_n.156, s32[]{:T(128)S(6)} %select_n.157) | dynamic-update-slice | bytes 32772 | tf_op jit(solution)/shard_map/while/body/eval_jaxpr/dynamic_update_slice | solution.py:73
  155.4 0.6 dynamic_slice.79
  157.9 0.6 dynamic_slice.80
  159.2 0.6 dynamic_slice.81
  161.8 5.4 %dynamic_update_slice.10 = f32[48,32,144]{2,1,0:T(8,128)S(1)} dynamic-update-slice(f32[48,32,144]{2,1,0:T(8,128)S(1)} %get-tuple-element.322, f32[16,16,16]{2,1,0:T(8,128)S(1)} %bitcast_add_fusion.2, s32[]{:T(128)S(6)} %select_n.154, s32[]{:T(128)S(6)} %select_n.156, s32[]{:T(128)S(6)} %select_n.157) | dynamic-update-slice | bytes 32772 | tf_op jit(solution)/shard_map/while/body/eval_jaxpr/dynamic_update_slice | solution.py:73
  167.4 0.6 dynamic_slice.79
  169.9 0.6 dynamic_slice.80
  171.2 0.6 dynamic_slice.81
  173.9 5.4 %dynamic_update_slice.10 = f32[48,32,144]{2,1,0:T(8,128)S(1)} dynamic-update-slice(f32[48,32,144]{2,1,0:T(8,128)S(1)} %get-tuple-element.322, f32[16,16,16]{2,1,0:T(8,128)S(1)} %bitcast_add_fusion.2, s32[]{:T(128)S(6)} %select_n.154, s32[]{:T(128)S(6)} %select_n.156, s32[]{:T(128)S(6)} %select_n.157) | dynamic-update-slice | bytes 32772 | tf_op jit(solution)/shard_map/while/body/eval_jaxpr/dynamic_update_slice | solution.py:73
  179.4 0.6 dynamic_slice.79
  182.0 0.6 dynamic_slice.80
  183.2 0.6 dynamic_slice.81
  185.9 5.4 %dynamic_update_slice.10 = f32[48,32,144]{2,1,0:T(8,128)S(1)} dynamic-update-slice(f32[48,32,144]{2,1,0:T(8,128)S(1)} %get-tuple-element.322, f32[16,16,16]{2,1,0:T(8,128)S(1)} %bitcast_add_fusion.2, s32[]{:T(128)S(6)} %select_n.154, s32[]{:T(128)S(6)} %select_n.156, s32[]{:T(128)S(6)} %select_n.157) | dynamic-update-slice | bytes 32772 | tf_op jit(solution)/shard_map/while/body/eval_jaxpr/dynamic_update_slice | solution.py:73
  191.5 0.6 dynamic_slice.79
  194.0 0.6 dynamic_slice.80
  195.2 0.6 dynamic_slice.81
  197.9 5.4 %dynamic_update_slice.10 = f32[48,32,144]{2,1,0:T(8,128)S(1)} dynamic-update-slice(f32[48,32,144]{2,1,0:T(8,128)S(1)} %get-tuple-element.322, f32[16,16,16]{2,1,0:T(8,128)S(1)} %bitcast_add_fusion.2, s32[]{:T(128)S(6)} %select_n.154, s32[]{:T(128)S(6)} %select_n.156, s32[]{:T(128)S(6)} %select_n.157) | dynamic-update-slice | bytes 32772 | tf_op jit(solution)/shard_map/while/body/eval_jaxpr/dynamic_update_slice | solution.py:73
  203.5 0.6 dynamic_slice.79
  206.0 0.6 dynamic_slice.80
  207.3 0.6 dynamic_slice.81
  209.9 5.4 %dynamic_update_slice.10 = f32[48,32,144]{2,1,0:T(8,128)S(1)} dynamic-update-slice(f32[48,32,144]{2,1,0:T(8,128)S(1)} %get-tuple-element.322, f32[16,16,16]{2,1,0:T(8,128)S(1)} %bitcast_add_fusion.2, s32[]{:T(128)S(6)} %select_n.154, s32[]{:T(128)S(6)} %select_n.156, s32[]{:T(128)S(6)} %select_n.157) | dynamic-update-slice | bytes 32772 | tf_op jit(solution)/shard_map/while/body/eval_jaxpr/dynamic_update_slice | solution.py:73
  215.5 0.6 dynamic_slice.79
  218.0 0.6 dynamic_slice.80
  219.3 0.6 dynamic_slice.81
  221.9 5.4 %dynamic_update_slice.10 = f32[48,32,144]{2,1,0:T(8,128)S(1)} dynamic-update-slice(f32[48,32,144]{2,1,0:T(8,128)S(1)} %get-tuple-element.322, f32[16,16,16]{2,1,0:T(8,128)S(1)} %bitcast_add_fusion.2, s32[]{:T(128)S(6)} %select_n.154, s32[]{:T(128)S(6)} %select_n.156, s32[]{:T(128)S(6)} %select_n.157) | dynamic-update-slice | bytes 32772 | tf_op jit(solution)/shard_map/while/body/eval_jaxpr/dynamic_update_slice | solution.py:73
  227.5 0.6 dynamic_slice.79
  230.1 0.6 dynamic_slice.80
  231.3 0.6 dynamic_slice.81
  234.0 5.4 %dynamic_update_slice.10 = f32[48,32,144]{2,1,0:T(8,128)S(1)} dynamic-update-slice(f32[48,32,144]{2,1,0:T(8,128)S(1)} %get-tuple-element.322, f32[16,16,16]{2,1,0:T(8,128)S(1)} %bitcast_add_fusion.2, s32[]{:T(128)S(6)} %select_n.154, s32[]{:T(128)S(6)} %select_n.156, s32[]{:T(128)S(6)} %select_n.157) | dynamic-update-slice | bytes 32772 | tf_op jit(solution)/shard_map/while/body/eval_jaxpr/dynamic_update_slice | solution.py:73
  239.6 2.0 scatter-add.6
  241.8 4.3 %collective-permute-done = bf16[16,32,128]{2,1,0:T(8,128)(2,1)S(1)} collective-permute-done((bf16[16,32,128]{2,1,0:T(8,128)(2,1)S(1)}, bf16[16,32,128]{2,1,0:T(8,128)(2,1)S(1)}, u32[]{:S(2)}, u32[]{:S(2)}) %collective-permute-start) | collective-permute-done | bytes 131104 | tf_op jit(solution)/shard_map/ppermute | solution.py:22
  246.2 7.7 %collective-permute-done.1 = bf16[32,16,128]{2,1,0:T(8,128)(2,1)S(1)} collective-permute-done((bf16[32,16,128]{2,1,0:T(8,128)(2,1)S(1)}, bf16[32,16,128]{2,1,0:T(8,128)(2,1)S(1)}, u32[]{:S(2)}, u32[]{:S(2)}) %collective-permute-start.1) | collective-permute-done | bytes 131104 | tf_op jit(solution)/shard_map/ppermute | solution.py:22
  253.9 0.7 slice_add_fusion.1
  (70 shorter events, 4.3 us)
Async XLA Ops:
  7.2 113.6 %copy-start = (f32[256]{0:T(256)S(1)}, f32[256]{0:T(256)}, u32[]{:S(2)}) copy-start(f32[256]{0:T(256)} %param.19) | copy-start | bytes 3076
  7.2 1.6 copy-start.6
  7.2 43.1 %all-reduce.5.cloned.1.call-start = ((), (), s32[]{:S(2)}) async-start(), calls=%async_computation | async-start | bytes 2097152 | tf_op jit(solution)/shard_map/psum | solution.py:16
  10.2 106.1 %all-reduce.7.cloned.1.call-start = ((), (), s32[]{:S(2)}) async-start(), calls=%async_computation.1 | async-start | bytes 4194304 | tf_op jit(solution)/shard_map/psum | solution.py:16
  11.7 0.7 copy-start.7
  116.3 1.6 copy-start.2
  116.3 3.0 %copy-start.1 = (bf16[512,512]{0,1:T(8,128)(2,1)S(1)}, bf16[512,512]{0,1:T(8,128)(2,1)}, u32[]{:S(2)}) copy-start(bf16[512,512]{0,1:T(8,128)(2,1)} %get-tuple-element.251) | copy-start | bytes 1572868
  116.3 3.0 %copy-start.4 = (bf16[512,256]{0,1:T(8,128)(2,1)S(1)}, bf16[512,256]{0,1:T(8,128)(2,1)}, u32[]{:S(2)}) copy-start(bf16[512,256]{0,1:T(8,128)(2,1)} %get-tuple-element.247) | copy-start | bytes 786436
  117.9 1.8 copy-start.3
  117.9 1.8 copy-start.5
  120.7 22.4 %copy-start.8 = (s32[8]{0:T(128)S(1)}, s32[8]{0:T(128)}, u32[]{:S(2)}) copy-start(s32[8]{0:T(128)} %param.21) | copy-start | bytes 100
  120.7 22.4 %copy-start.9 = (s32[8]{0:T(128)S(1)}, s32[8]{0:T(128)}, u32[]{:S(2)}) copy-start(s32[8]{0:T(128)} %param.22) | copy-start | bytes 100
  120.7 22.5 %copy-start.10 = (s32[8]{0:T(128)S(1)}, s32[8]{0:T(128)}, u32[]{:S(2)}) copy-start(s32[8]{0:T(128)} %param.23) | copy-start | bytes 100
  241.7 4.4 %collective-permute-start = (bf16[16,32,128]{2,1,0:T(8,128)(2,1)S(1)}, bf16[16,32,128]{2,1,0:T(8,128)(2,1)S(1)}, u32[]{:S(2)}, u32[]{:S(2)}) collective-permute-start(bf16[16,32,128]{2,1,0:T(8,128)(2,1)S(1)} %slice.111), channel_id=1, source_target_pairs={{24,0},{0,8},{8,16},{16,24},{25,1},{1,9},{9,17},{17,25},{26,2},{2,... | collective-permute-start | bytes 393224 | tf_op jit(solution)/shard_map/ppermute | solution.py:22
  246.2 7.7 %collective-permute-start.1 = (bf16[32,16,128]{2,1,0:T(8,128)(2,1)S(1)}, bf16[32,16,128]{2,1,0:T(8,128)(2,1)S(1)}, u32[]{:S(2)}, u32[]{:S(2)}) collective-permute-start(bf16[32,16,128]{2,1,0:T(8,128)(2,1)S(1)} %slice.110), channel_id=1, source_target_pairs={{7,0},{0,1},{1,2},{2,3},{3,4},{4,5},{5,6},{6,7},{15,8},{8,9},{9,10... | collective-permute-start | bytes 393224 | tf_op jit(solution)/shard_map/ppermute | solution.py:22
Sparse Core Ops, SparseCore 0:
  11.1 39.1 all-reduce.4
  52.8 63.5 all-reduce.6
where the time goes:
time: 262 us; the launch traced here: 261 us
  waiting for transfers between devices  116 us (44%)
  local copies, waits for them, and re-layouts  63.4 us (24%)
  loops' own time  36.8 us (14%)
  blocking collectives  20.6 us (8%)
  between operations  14.3 us (5%)
  matrix products  5.91 us (2%)
  other arithmetic  4.43 us (2%)
    psum x2, waiting for transfers between devices, broadcast(): return lax.psum(block, axis)  104 us
    dynamic_update_slice x8, local copies, waits for them, and re-layouts, deposit(): lax.dynamic_update_slice(buffer, current + weight * tile_values, (start_x...  43.1 us
    another operation x1, loops' own time, local(): lax.fori_loop(0, atom_count, deposit, jnp.zeros((SX + TILE, SY + TILE, GZ...  36.8 us
    psum x1, blocking collectives, local(): charges = lax.psum(partial_charges, ('col', 'layer'))  20.6 us
    ppermute x2, waiting for transfers between devices, shifted(): return lax.ppermute(block, axis, route)  12 us
  transfers between devices with their start and end apart: 4, of which 4 were waited for; matrix products, arithmetic and copies ran while one was open for 1% of the time, Pallas kernels for 0%

commit v1 on v0

--- a/solution.py
+++ b/solution.py
@@ -25,6 +25,11 @@
 def local(
     density_matrix, block_mask, intersection_weights, exponents, anchor_x, anchor_y, anchor_z
 ):
+
+    def shape_units(x0, axis_tag):
+        block_last = lax.all_gather(x0, axis_tag).sum(axis=0)
+        return block_last
+
     row_count = lax.axis_size("row")
     col_count = lax.axis_size("col")
     layer_count = lax.axis_size("layer")
@@ -44,7 +49,7 @@
         running = running + jnp.dot(left_part, right_part, preferred_element_type=jnp.float32)
     squared = running.astype(jnp.bfloat16)
     partial_charges = jnp.dot(running, intersection_weights, precision=lax.Precision.HIGHEST)
-    charges = lax.psum(partial_charges, ("col", "layer"))
+    charges = shape_units(partial_charges, ("col", "layer"))
     atom_count = anchor_x.shape[0]
     y_index = lax.axis_index("col") * layer_count + layer_at
     offsets = jnp.arange(TILE, dtype=jnp.int32)

time: 262 us -> 269 us (1.027)
  blocking collectives: 20.6 us -> 27 us
    all_gather x0 -> x1, blocking collectives: none -> 27 us  [shape_units(): block_last = lax.all_gather(x0, axis_tag).sum(axis=0)]
    psum x1 -> x0, blocking collectives: 20.6 us -> none  [local(): charges = lax.psum(partial_charges, ('col', 'layer'))]
where the time goes in v1:
time: 269 us; the launch traced here: 268 us
  waiting for transfers between devices  115 us (43%)
  local copies, waits for them, and re-layouts  63.4 us (24%)
  loops' own time  36.8 us (14%)
  blocking collectives  27 us (10%)
  between operations  14.3 us (5%)
  matrix products  5.91 us (2%)
  other arithmetic  4.46 us (2%)
    psum x2, waiting for transfers between devices, broadcast(): return lax.psum(block, axis)  104 us
    dynamic_update_slice x8, local copies, waits for them, and re-layouts, deposit(): lax.dynamic_update_slice(buffer, current + weight * tile_values, (start_x...  43.1 us
    another operation x1, loops' own time, local(): lax.fori_loop(0, atom_count, deposit, jnp.zeros((SX + TILE, SY + TILE, GZ...  36.8 us
    all_gather x1, blocking collectives, shape_units(): block_last = lax.all_gather(x0, axis_tag).sum(axis=0)  27 us
    ppermute x2, waiting for transfers between devices, shifted(): return lax.ppermute(block, axis, route)  11.4 us
  transfers between devices with their start and end apart: 4, of which 4 were waited for; matrix products, arithmetic and copies ran while one was open for 1% of the time, Pallas kernels for 0%

profile of v1, /device:TPU:0, one launch (start us, length us, event | category | flops | bytes accessed | tf_op | source)
XLA Modules:
  0.0 268.0 jit_solution(16348250379827280773)
XLA Ops:
  7.2 1.5 copy.14
  9.2 1.1 broadcast_select_fusion.4
  10.3 1.4 broadcast_select_fusion
  11.7 0.6 copy-done.7
  12.5 37.8 %all-reduce.5.cloned.1.call-done = (bf16[512,256]{0,1:T(8,128)(2,1)}, bf16[512,256]{0,1:T(8,128)(2,1)}, bf16[512,256]{0,1:T(8,128)(2,1)}, bf16[512,256]{0,1:T(8,128)(2,1)}) async-done(((bf16[512,256]{0,1:T(8,128)(2,1)}, bf16[512,256]{0,1:T(8,128)(2,1)}, bf16[512,256]{0,1:T(8,128)(2,1)}, bf16[512,256]{0,1:T(8,128)(2,1)}), (bf16[512,256]{0,1:T(8,128)(2,1)}, bf16[512,256]{0,1:T(8,128)(2,1)}, ...) | async-done | bytes 1048592 | tf_op jit(solution)/shard_map/psum | solution.py:16
  50.3 66.0 %all-reduce.7.cloned.1.call-done = (bf16[512,512]{0,1:T(8,128)(2,1)}, bf16[512,512]{0,1:T(8,128)(2,1)}, bf16[512,512]{0,1:T(8,128)(2,1)}, bf16[512,512]{0,1:T(8,128)(2,1)}) async-done(((bf16[512,512]{0,1:T(8,128)(2,1)}, bf16[512,512]{0,1:T(8,128)(2,1)}, bf16[512,512]{0,1:T(8,128)(2,1)}, bf16[512,512]{0,1:T(8,128)(2,1)}), (bf16[512,512]{0,1:T(8,128)(2,1)}, bf16[512,512]{0,1:T(8,128)(2,1)}, ...) | async-done | bytes 2097168 | tf_op jit(solution)/shard_map/psum | solution.py:16
  116.3 1.6 fusion.8
  117.9 1.4 convolution_add_fusion.2
  119.7 1.0 fusion.7
  121.3 27.0 %all-gather.1 = f32[8,1,512]{2,1,0:T(1,128)S(1)} all-gather(f32[1,1,512]{2,1,0:T(1,128)S(1)} %convolution_bitcast_fusion.1), channel_id=2, replica_groups=mesh['row'=4,'col'=2,'layer'=4] {'col','layer'}, dimensions={0}, use_global_device_ids=true | all-gather | bytes 18432 | tf_op jit(solution)/shard_map/all_gather | solution.py:30
  148.4 1.1 convolution_bitcast_fusion
  149.7 96.2 %while.19 = (s32[]{:T(128)}, f32[48,32,144]{2,1,0:T(8,128)S(1)}, s32[8]{0:T(128)S(1)}, s32[8]{0:T(128)S(1)}, s32[]{:T(128)}, /*index=5*/s32[8]{0:T(128)S(1)}, f3...) while((s32[]{:T(128)}, f32[48,32,144]{2,1,0:T(8,128)S(1)}, ...), condition=%wide.region_10.11_spmd, body=%wide.region_9.10_spmd.sunk | while | flops 8209 | bytes 147826 | solution.py:82
  149.9 0.6 dynamic_slice.79
  152.4 0.6 dynamic_slice.80
  153.7 0.6 dynamic_slice.81
  156.3 5.4 %dynamic_update_slice.10 = f32[48,32,144]{2,1,0:T(8,128)S(1)} dynamic-update-slice(f32[48,32,144]{2,1,0:T(8,128)S(1)} %get-tuple-element.329, f32[16,16,16]{2,1,0:T(8,128)S(1)} %bitcast_add_fusion.2, s32[]{:T(128)S(6)} %select_n.154, s32[]{:T(128)S(6)} %select_n.156, s32[]{:T(128)S(6)} %select_n.157) | dynamic-update-slice | bytes 32772 | tf_op jit(solution)/shard_map/while/body/eval_jaxpr/dynamic_update_slice | solution.py:78
  161.9 0.6 dynamic_slice.79
  164.4 0.6 dynamic_slice.80
  165.7 0.6 dynamic_slice.81
  168.4 5.4 %dynamic_update_slice.10 = f32[48,32,144]{2,1,0:T(8,128)S(1)} dynamic-update-slice(f32[48,32,144]{2,1,0:T(8,128)S(1)} %get-tuple-element.329, f32[16,16,16]{2,1,0:T(8,128)S(1)} %bitcast_add_fusion.2, s32[]{:T(128)S(6)} %select_n.154, s32[]{:T(128)S(6)} %select_n.156, s32[]{:T(128)S(6)} %select_n.157) | dynamic-update-slice | bytes 32772 | tf_op jit(solution)/shard_map/while/body/eval_jaxpr/dynamic_update_slice | solution.py:78
  173.9 0.6 dynamic_slice.79
  176.5 0.6 dynamic_slice.80
  177.7 0.6 dynamic_slice.81
  180.4 5.4 %dynamic_update_slice.10 = f32[48,32,144]{2,1,0:T(8,128)S(1)} dynamic-update-slice(f32[48,32,144]{2,1,0:T(8,128)S(1)} %get-tuple-element.329, f32[16,16,16]{2,1,0:T(8,128)S(1)} %bitcast_add_fusion.2, s32[]{:T(128)S(6)} %select_n.154, s32[]{:T(128)S(6)} %select_n.156, s32[]{:T(128)S(6)} %select_n.157) | dynamic-update-slice | bytes 32772 | tf_op jit(solution)/shard_map/while/body/eval_jaxpr/dynamic_update_slice | solution.py:78
  185.9 0.6 dynamic_slice.79
  188.5 0.6 dynamic_slice.80
  189.7 0.6 dynamic_slice.81
  192.4 5.4 %dynamic_update_slice.10 = f32[48,32,144]{2,1,0:T(8,128)S(1)} dynamic-update-slice(f32[48,32,144]{2,1,0:T(8,128)S(1)} %get-tuple-element.329, f32[16,16,16]{2,1,0:T(8,128)S(1)} %bitcast_add_fusion.2, s32[]{:T(128)S(6)} %select_n.154, s32[]{:T(128)S(6)} %select_n.156, s32[]{:T(128)S(6)} %select_n.157) | dynamic-update-slice | bytes 32772 | tf_op jit(solution)/shard_map/while/body/eval_jaxpr/dynamic_update_slice | solution.py:78
  198.0 0.6 dynamic_slice.79
  200.5 0.6 dynamic_slice.80
  201.8 0.6 dynamic_slice.81
  204.4 5.4 %dynamic_update_slice.10 = f32[48,32,144]{2,1,0:T(8,128)S(1)} dynamic-update-slice(f32[48,32,144]{2,1,0:T(8,128)S(1)} %get-tuple-element.329, f32[16,16,16]{2,1,0:T(8,128)S(1)} %bitcast_add_fusion.2, s32[]{:T(128)S(6)} %select_n.154, s32[]{:T(128)S(6)} %select_n.156, s32[]{:T(128)S(6)} %select_n.157) | dynamic-update-slice | bytes 32772 | tf_op jit(solution)/shard_map/while/body/eval_jaxpr/dynamic_update_slice | solution.py:78
  210.0 0.6 dynamic_slice.79
  212.5 0.6 dynamic_slice.80
  213.8 0.6 dynamic_slice.81
  216.4 5.4 %dynamic_update_slice.10 = f32[48,32,144]{2,1,0:T(8,128)S(1)} dynamic-update-slice(f32[48,32,144]{2,1,0:T(8,128)S(1)} %get-tuple-element.329, f32[16,16,16]{2,1,0:T(8,128)S(1)} %bitcast_add_fusion.2, s32[]{:T(128)S(6)} %select_n.154, s32[]{:T(128)S(6)} %select_n.156, s32[]{:T(128)S(6)} %select_n.157) | dynamic-update-slice | bytes 32772 | tf_op jit(solution)/shard_map/while/body/eval_jaxpr/dynamic_update_slice | solution.py:78
  222.0 0.6 dynamic_slice.79
  224.5 0.6 dynamic_slice.80
  225.8 0.6 dynamic_slice.81
  228.5 5.4 %dynamic_update_slice.10 = f32[48,32,144]{2,1,0:T(8,128)S(1)} dynamic-update-slice(f32[48,32,144]{2,1,0:T(8,128)S(1)} %get-tuple-element.329, f32[16,16,16]{2,1,0:T(8,128)S(1)} %bitcast_add_fusion.2, s32[]{:T(128)S(6)} %select_n.154, s32[]{:T(128)S(6)} %select_n.156, s32[]{:T(128)S(6)} %select_n.157) | dynamic-update-slice | bytes 32772 | tf_op jit(solution)/shard_map/while/body/eval_jaxpr/dynamic_update_slice | solution.py:78
  234.0 0.6 dynamic_slice.79
  237.8 0.6 dynamic_slice.81
  240.5 5.4 %dynamic_update_slice.10 = f32[48,32,144]{2,1,0:T(8,128)S(1)} dynamic-update-slice(f32[48,32,144]{2,1,0:T(8,128)S(1)} %get-tuple-element.329, f32[16,16,16]{2,1,0:T(8,128)S(1)} %bitcast_add_fusion.2, s32[]{:T(128)S(6)} %select_n.154, s32[]{:T(128)S(6)} %select_n.156, s32[]{:T(128)S(6)} %select_n.157) | dynamic-update-slice | bytes 32772 | tf_op jit(solution)/shard_map/while/body/eval_jaxpr/dynamic_update_slice | solution.py:78
  246.1 2.0 scatter-add.6
  248.3 4.3 %collective-permute-done = bf16[16,32,128]{2,1,0:T(8,128)(2,1)S(1)} collective-permute-done((bf16[16,32,128]{2,1,0:T(8,128)(2,1)S(1)}, bf16[16,32,128]{2,1,0:T(8,128)(2,1)S(1)}, u32[]{:S(2)}, u32[]{:S(2)}) %collective-permute-start) | collective-permute-done | bytes 131104 | tf_op jit(solution)/shard_map/ppermute | solution.py:22
  252.7 0.6 collective-permute-start.1
  253.3 7.1 %collective-permute-done.1 = bf16[32,16,128]{2,1,0:T(8,128)(2,1)S(1)} collective-permute-done((bf16[32,16,128]{2,1,0:T(8,128)(2,1)S(1)}, bf16[32,16,128]{2,1,0:T(8,128)(2,1)S(1)}, u32[]{:S(2)}, u32[]{:S(2)}) %collective-permute-start.1) | collective-permute-done | bytes 131104 | tf_op jit(solution)/shard_map/ppermute | solution.py:22
  260.4 0.7 slice_add_fusion.1
  (71 shorter events, 4.9 us)
Async XLA Ops:
  7.2 113.6 %copy-start = (f32[256]{0:T(256)S(1)}, f32[256]{0:T(256)}, u32[]{:S(2)}) copy-start(f32[256]{0:T(256)} %param.19) | copy-start | bytes 3076
  7.2 1.6 copy-start.6
  7.2 43.1 %all-reduce.5.cloned.1.call-start = ((), (), s32[]{:S(2)}) async-start(), calls=%async_computation | async-start | bytes 2097152 | tf_op jit(solution)/shard_map/psum | solution.py:16
  10.2 106.1 %all-reduce.7.cloned.1.call-start = ((), (), s32[]{:S(2)}) async-start(), calls=%async_computation.1 | async-start | bytes 4194304 | tf_op jit(solution)/shard_map/psum | solution.py:16
  11.7 0.7 copy-start.7
  116.3 1.6 copy-start.2
  116.3 3.0 %copy-start.1 = (bf16[512,512]{0,1:T(8,128)(2,1)S(1)}, bf16[512,512]{0,1:T(8,128)(2,1)}, u32[]{:S(2)}) copy-start(bf16[512,512]{0,1:T(8,128)(2,1)} %get-tuple-element.258) | copy-start | bytes 1572868
  116.3 3.0 %copy-start.4 = (bf16[512,256]{0,1:T(8,128)(2,1)S(1)}, bf16[512,256]{0,1:T(8,128)(2,1)}, u32[]{:S(2)}) copy-start(bf16[512,256]{0,1:T(8,128)(2,1)} %get-tuple-element.254) | copy-start | bytes 786436
  117.9 1.8 copy-start.3
  117.9 1.8 copy-start.5
  120.7 28.9 %copy-start.8 = (s32[8]{0:T(128)S(1)}, s32[8]{0:T(128)}, u32[]{:S(2)}) copy-start(s32[8]{0:T(128)} %param.21) | copy-start | bytes 100
  120.7 29.0 %copy-start.9 = (s32[8]{0:T(128)S(1)}, s32[8]{0:T(128)}, u32[]{:S(2)}) copy-start(s32[8]{0:T(128)} %param.22) | copy-start | bytes 100
  120.7 29.0 %copy-start.10 = (s32[8]{0:T(128)S(1)}, s32[8]{0:T(128)}, u32[]{:S(2)}) copy-start(s32[8]{0:T(128)} %param.23) | copy-start | bytes 100
  248.2 4.4 %collective-permute-start = (bf16[16,32,128]{2,1,0:T(8,128)(2,1)S(1)}, bf16[16,32,128]{2,1,0:T(8,128)(2,1)S(1)}, u32[]{:S(2)}, u32[]{:S(2)}) collective-permute-start(bf16[16,32,128]{2,1,0:T(8,128)(2,1)S(1)} %slice.111), channel_id=1, source_target_pairs={{24,0},{0,8},{8,16},{16,24},{25,1},{1,9},{9,17},{17,25},{26,2},{2,... | collective-permute-start | bytes 393224 | tf_op jit(solution)/shard_map/ppermute | solution.py:22
  252.7 7.7 %collective-permute-start.1 = (bf16[32,16,128]{2,1,0:T(8,128)(2,1)S(1)}, bf16[32,16,128]{2,1,0:T(8,128)(2,1)S(1)}, u32[]{:S(2)}, u32[]{:S(2)}) collective-permute-start(bf16[32,16,128]{2,1,0:T(8,128)(2,1)S(1)} %slice.110), channel_id=1, source_target_pairs={{7,0},{0,1},{1,2},{2,3},{3,4},{4,5},{5,6},{6,7},{15,8},{8,9},{9,10... | collective-permute-start | bytes 393224 | tf_op jit(solution)/shard_map/ppermute | solution.py:22
Sparse Core Ops, SparseCore 0:
  11.1 39.1 all-reduce.4
  52.8 63.5 all-reduce.6
